TPU v7x, 256 devices: a whole 4x4x8 slice. The times are simulated.
256 devices in a mesh: tm: 32 (over y_hi, z, core), head: 4 (over x), rep: 2 (over y_lo).
Axes of the slice: x: 4, y: 4 (y_hi: 2, y_lo: 2; y = y_hi * 2 + y_lo), z: 8, core: 2. Of those that a mesh axis runs over, the one named last changes fastest.
Arguments:
- queries: bfloat16 [32768, 1536], P(('tm', 'rep'), 'head'), may hold values from -8 to 8
- kv_cache: bfloat16 [32768, 2, 1536], P('tm', None, 'head'), may hold values from -8 to 8
- out_weight: bfloat16 [1536, 3072], P('head'), may hold values from -0.15625 to 0.15625
- fetch_list: int32 [64, 32], P(('tm', 'rep')), may hold values from 0 to 247, as said below
- tile_lists: int32 [256, 16], P(('tm', 'rep')), may hold values from 0 to 31, as said below
- event_offsets: int32 [256], P(('tm', 'rep')), may hold values from 0 to 7
Outputs:
- mixed: bfloat16 [32768, 3072], P(('tm', 'rep'), 'head')
Inputs may be any that keep to these rules, and one draw needn't show every extreme that they name: `fetch_list`: each row names 32 distinct blocks, all with ids below (31) * 8, so none of the newest ones; one row names at most 2 blocks of one owner, and every row names exactly 2 blocks of some owner. `tile_lists`: each row names 16 distinct positions; the tiles of one device together name every position of its row of fetch_list.
All inputs are finite; a program needn't handle non-finite values.
Results may differ from a plain program's by a relative error of at most 0.013.
Values may be sent and summed in bfloat16 or wider, within the bound.
No kernel may reach another device: no remote copies, remote signals or barrier semaphores. Data moves between devices by JAX's collectives and lax.ppermute only.
A program may use at most 128 MiB of HBM per device.

v0:
```python
import math
import jax
import jax.numpy as jnp
from jax import lax
from jax.sharding import PartitionSpec as P

DH = 128
TILE = 128
CB_DEV = 8
CAP = 2


def from_root(shard, axis, root):
    mine = lax.axis_index(axis) == root
    return lax.psum(jnp.where(mine, shard, jnp.zeros_like(shard)), axis)


def owner_ranks(owners):
    entry_count = owners.shape[-1]
    index_row = jnp.arange(entry_count, dtype=jnp.int32)
    same_owner = owners[..., None, :] == owners[..., :, None]
    earlier = index_row[None, :] < index_row[:, None]
    return jnp.sum(same_owner & earlier, axis=-1)


def outgoing(requests, wanted, block_rows, me_owner):
    owners = requests // CB_DEV
    slot_ids = requests % CB_DEV
    rank_ids = owner_ranks(owners)
    is_mine = owners == me_owner
    hit_table = is_mine[:, :, None] & (rank_ids[:, :, None] == wanted[None, None, :])
    chosen = jnp.sum(jnp.where(hit_table, slot_ids[:, :, None], 0), axis=1)
    in_use = jnp.any(hit_table, axis=1)
    picked = jnp.take(block_rows, chosen, axis=0)
    return jnp.where(in_use[:, :, None, None, None], picked, jnp.zeros_like(picked))


def shards(queries, kv_cache, out_weight, fetch_list, tile_lists, event_offsets):
    me_owner = lax.axis_index("tm")
    feature_width = kv_cache.shape[2]
    head_count = feature_width // DH
    block_rows = kv_cache.reshape(CB_DEV, -1, 2, feature_width)
    block_len = block_rows.shape[1]
    own_owners = fetch_list[0] // CB_DEV
    own_ranks = owner_ranks(own_owners)
    requests = lax.all_gather(fetch_list, "tm", axis=0, tiled=True)
    outbound = outgoing(requests, jnp.arange(CAP, dtype=jnp.int32), block_rows, me_owner)
    arrived = lax.all_to_all(outbound, "tm", split_axis=0, concat_axis=0, tiled=True)
    flat_blocks = arrived.reshape(-1, block_len, 2, feature_width)
    fetched = jnp.take(flat_blocks, own_owners * CAP + own_ranks, axis=0)
    newest = lax.axis_size("tm") - 1
    panel_rows = from_root(kv_cache, "tm", newest)
    panel_keys = panel_rows[:, 0].reshape(-1, head_count, DH)
    panel_values = panel_rows[:, 1].reshape(-1, head_count, DH)
    slab_rows = panel_keys.shape[0]
    tile_count = queries.shape[0] // TILE
    per_step = math.gcd(tile_count, 4)
    query_groups = queries.reshape(tile_count // per_step, per_step, TILE, head_count, DH)
    list_groups = tile_lists.reshape(tile_count // per_step, per_step, -1)
    offset_groups = event_offsets.reshape(tile_count // per_step, per_step)
    score_scale = 1.0 / math.sqrt(DH)
    positions = jnp.arange(slab_rows, dtype=jnp.int32)

    def attend(pieces):
        query_block, list_rows, offsets = pieces
        picked = jnp.take(fetched, list_rows, axis=0).reshape(per_step, -1, 2, feature_width)
        far_keys = picked[:, :, 0].reshape(per_step, -1, head_count, DH)
        far_values = picked[:, :, 1].reshape(per_step, -1, head_count, DH)
        far_scores = (
            jnp.einsum("gqhd,gkhd->ghqk", query_block, far_keys, preferred_element_type=jnp.float32)
            * score_scale
        )
        near_scores = (
            jnp.einsum(
                "gqhd,khd->ghqk", query_block, panel_keys, preferred_element_type=jnp.float32
            )
            * score_scale
        )
        visible = positions[None, :] < (CB_DEV - offsets)[:, None] * block_len
        near_scores = jnp.where(visible[:, None, None, :], near_scores, -1e30)
        row_max = jnp.maximum(jnp.max(far_scores, axis=-1), jnp.max(near_scores, axis=-1))
        far_weights = jnp.exp(far_scores - row_max[..., None])
        near_weights = jnp.exp(near_scores - row_max[..., None])
        denom_sum = jnp.sum(far_weights, axis=-1) + jnp.sum(near_weights, axis=-1)
        blended = jnp.einsum(
            "ghqk,gkhd->gqhd",
            far_weights.astype(jnp.bfloat16),
            far_values,
            preferred_element_type=jnp.float32,
        )
        blended = blended + jnp.einsum(
            "ghqk,khd->gqhd",
            near_weights.astype(jnp.bfloat16),
            panel_values,
            preferred_element_type=jnp.float32,
        )
        blended = blended / jnp.transpose(denom_sum, (0, 2, 1))[..., None]
        return blended.astype(jnp.bfloat16).reshape(per_step, TILE, head_count * DH)

    attended = lax.map(attend, (query_groups, list_groups, offset_groups)).reshape(
        -1, head_count * DH
    )
    partial_value = jnp.dot(attended, out_weight, preferred_element_type=jnp.float32)
    return lax.psum_scatter(
        partial_value.astype(jnp.bfloat16), "head", scatter_dimension=1, tiled=True
    )


def solution(mesh):
    placed = (
        P(("tm", "rep"), "head"),
        P("tm", None, "head"),
        P("head", None),
        P(("tm", "rep"), None),
        P(("tm", "rep"), None),
        P(("tm", "rep")),
    )
    return jax.shard_map(
        shards, mesh=mesh, in_specs=placed, out_specs=P(("tm", "rep"), "head"), check_vma=False
    )
```

profile of v0, /device:TPU:1, one launch (start us, length us, event | category | flops | bytes accessed | tf_op | source)
XLA Modules:
  0.0 600.0 jit_solution(15882582718426881978)
XLA Ops:
  6.5 46.3 %all-gather = s32[32,1,32]{2,1,0:T(1,128)S(1)} all-gather(s32[1,1,32]{2,1,0:T(1,128)} %bitcast.112), channel_id=1, replica_groups=mesh['tm'=32,'head'=4,'rep'=2] {'tm'}, dimensions={0}, use_global_device_ids=true | all-gather | bytes 4224 | tf_op jit(solution)/shard_map/all_gather | solution.py:46
  52.9 0.8 convert_reduce_fusion
  53.6 0.1 select_reduce_fusion
  53.8 0.1 fusion.34
  53.9 0.1 copy.118
  54.0 0.1 reshape.205
  54.1 29.4 %gather_fusion = bf16[64,128,2,384]{3,2,1,0:T(2,128)(2,1)} fusion(bf16[8,128,2,384]{3,2,1,0:T(2,128)(2,1)} %bitcast.101, s32[1024]{0:T(1024)S(1)} %pad_clamp_fusion.2), kind=kCustom, calls=%fused_computation | custom fusion | bytes 25166080 | tf_op jit(solution)/shard_map/jit(_take)/gather | solution.py:34
  83.5 11.5 %copy.119 = bf16[64,128,2,384]{3,1,2,0:T(8,128)(2,1)} copy(bf16[64,128,2,384]{3,2,1,0:T(2,128)(2,1)} %gather_fusion) | data formatting | bytes 25165824 | tf_op jit(solution)/shard_map/jit(_take)/gather | solution.py:34
  95.0 0.1 copy.117
  95.2 0.1 copy.116
  95.3 11.0 %select_select_fusion = bf16[32,2,128,2,384]{4,2,3,1,0:T(8,128)(2,1)} fusion(bf16[32,2,128,2,384]{4,2,3,1,0:T(8,128)(2,1)} %bitcast.102, pred[32,2]{1,0:T(8,128)(4,1)S(1)} %copy.117, pred[32,2]{1,0:T(8,128)(4,1)S(1)} %copy.116), kind=kLoop, calls=%fused_computation.7 | loop fusion | flops 12582912 | bytes 25165952 | tf_op jit(solution)/shard_map/jit(_where)/select_n | solution.py:35
  106.3 4.8 all-to-all-start
  111.2 0.0 copy-start.3
  111.2 0.0 copy-start.1
  111.2 0.0 copy-start.4
  111.2 0.0 all-reduce.2.cloned.1.call-start
  111.3 5.0 copy.126
  116.3 1.3 broadcast_select_fusion.1
  117.6 0.0 all-reduce.2.cloned.1.call-update
  117.6 0.0 reduce-scatter.2.cloned.1.call-start
  117.6 0.1 broadcast_bitcast_fusion
  117.8 0.1 reshape.221
  117.8 0.2 copy.123
  118.0 0.1 squeeze.28
  118.2 0.2 convert_reduce_fusion.1
  118.4 0.6 pad_clamp_fusion.1
  119.0 0.6 compare_and_fusion.1
  119.6 0.1 iota_compare_fusion.1
  119.7 346.7 %all-reduce.2.cloned.1.call-done = bf16[1024,2,384]{0,2,1:T(8,128)(2,1)} async-done(((bf16[1024,2,384]{0,2,1:T(8,128)(2,1)}), bf16[1024,2,384]{0,2,1:T(8,128)(2,1)}) %all-reduce.2.cloned.1.call-update) | async-done | bytes 1572880 | tf_op jit(solution)/shard_map/psum | solution.py:15
  466.4 1.5 fusion.42
  467.9 4.3 fusion.9
  472.2 8.7 %gather_fusion.1 = bf16[32,128,2,384]{3,1,2,0:T(8,128)(2,1)} fusion(bf16[64,128,2,384]{3,1,2,0:T(8,128)(2,1)} %bitcast.7, s32[1024]{0:T(1024)} %pad_clamp_fusion.1), kind=kCustom, calls=%fused_computation.1 | custom fusion | bytes 12583040 | tf_op jit(solution)/shard_map/jit(_take)/gather | solution.py:50
  480.9 6.2 %broadcast_select_fusion = bf16[32,128,2,384]{3,1,2,0:T(8,128)(2,1)} fusion(bf16[32,128,2,384]{3,1,2,0:T(8,128)(2,1)} %gather_fusion.1, pred[32]{0:T(512)(128)(4,1)} %compare_and_fusion.1), kind=kLoop, calls=%fused_computation.15 | loop fusion | flops 3145728 | bytes 12582944 | tf_op jit(solution)/shard_map/jit(_take)/select_n | solution.py:50
  487.1 9.9 %gather_fusion.2 = bf16[64,128,2,384]{3,1,2,0:T(8,128)(2,1)} fusion(bf16[32,128,2,384]{3,1,2,0:T(8,128)(2,1)} %broadcast_select_fusion, s32[1024]{0:T(1024)S(1)} %pad_clamp_fusion), kind=kCustom, calls=%fused_computation.2 | custom fusion | bytes 25166080 | tf_op jit(solution)/shard_map/while/body/eval_jaxpr/jit(_take)/gather | solution.py:66
  496.9 7.0 %copy.120 = bf16[64,128,2,384]{3,1,0,2:T(8,128)(2,1)S(1)} copy(bf16[64,128,2,384]{3,1,2,0:T(8,128)(2,1)} %gather_fusion.2) | data formatting | bytes 25165824 | tf_op jit(solution)/shard_map/while/body/eval_jaxpr/jit(_take)/gather | solution.py:66
  504.0 3.0 bitcast_select_fusion
  506.9 5.7 fusion.41
  512.7 8.7 %copy.121 = bf16[4,2048,1,384]{1,3,0,2:T(8,128)(2,1)} copy(bf16[4,2048,1,384]{3,1,0,2:T(8,128)(2,1)} %get-tuple-element.24) | data formatting | bytes 12582912 | tf_op jit(solution)/shard_map/while/body/eval_jaxpr/slice | solution.py:68
  521.3 8.6 %copy.122 = bf16[4,2048,1,384]{1,3,0,2:T(8,128)(2,1)} copy(bf16[4,2048,1,384]{3,1,0,2:T(8,128)(2,1)} %get-tuple-element.23) | data formatting | bytes 12582912 | tf_op jit(solution)/shard_map/while/body/eval_jaxpr/slice | solution.py:67
  529.9 4.7 bitcast_reduce_fusion
  534.6 2.1 fusion.1
  536.7 5.4 fusion.12
  542.1 4.7 fusion.7
  546.9 0.6 fusion.24
  547.5 0.3 copy.134
  547.9 3.5 convolution_convert_fusion
  551.4 0.0 reduce-scatter.2.cloned.1.call-update
  551.4 41.8 %reduce-scatter.2.cloned.1.call-done = bf16[512,768]{1,0:T(8,128)(2,1)} async-done(((bf16[512,3072]{1,0:T(8,128)(2,1)}), bf16[512,768]{1,0:T(8,128)(2,1)}) %reduce-scatter.2.cloned.1.call-update) | async-done | bytes 786448 | tf_op jit(solution)/shard_map/reduce_scatter | solution.py:104
  (27 shorter events, 0.2 us)
Async XLA Ops:
  6.5 541.3 %copy-start = (bf16[384,3072]{1,0:T(8,128)(2,1)S(1)}, bf16[384,3072]{1,0:T(8,128)(2,1)}, u32[]{:S(2)}) copy-start(bf16[384,3072]{1,0:T(8,128)(2,1)} %param.8) | copy-start | bytes 7077892
  106.3 365.9 %all-to-all-start = ((bf16[32,2,128,2,384]{4,2,3,1,0:T(8,128)(2,1)}), bf16[32,2,128,2,384]{4,2,3,1,0:T(8,128)(2,1)}, u32[]{:S(2)}, u32[]{:S(2)}) async-start(bf16[32,2,128,2,384]{4,2,3,1,0:T(8,128)(2,1)} %select_select_fusion), calls=%async_computation | async-start | bytes 25165824 | tf_op jit(solution)/shard_map/all_to_all | solution.py:48
  111.2 6.5 %copy-start.3 = (s32[4,16]{1,0:T(4,128)S(1)}, s32[4,16]{1,0:T(4,128)}, u32[]{:S(2)}) copy-start(s32[4,16]{1,0:T(4,128)} %param.10) | copy-start | bytes 772
  111.2 6.7 %copy-start.1 = (bf16[512,384]{1,0:T(8,128)(2,1)S(1)}, bf16[512,384]{1,0:T(8,128)(2,1)}, u32[]{:S(2)}) copy-start(bf16[512,384]{1,0:T(8,128)(2,1)} %param.6) | copy-start | bytes 1179652
  111.2 7.0 %copy-start.4 = (s32[1,32]{1,0:T(1,128)S(1)}, s32[1,32]{1,0:T(1,128)}, u32[]{:S(2)}) copy-start(s32[1,32]{1,0:T(1,128)} %param.9) | copy-start | bytes 388
  111.2 7.8 %copy-start.5 = (s32[4]{0:T(128)S(1)}, s32[4]{0:T(128)}, u32[]{:S(2)}) copy-start(s32[4]{0:T(128)} %param.11) | copy-start | bytes 52
  111.2 355.2 %all-reduce.2.cloned.1.call-start = ((), (), s32[]{:S(2)}) async-start(), calls=%async_computation.2 | async-start | bytes 3145728 | tf_op jit(solution)/shard_map/psum | solution.py:15
  117.6 475.6 %reduce-scatter.2.cloned.1.call-start = ((), (), s32[]{:S(2)}) async-start(), calls=%async_computation.3 | async-start | bytes 3932160 | tf_op jit(solution)/shard_map/reduce_scatter | solution.py:104
  529.9 4.7 copy-start.2
Sparse Core Ops, SparseCore 0:
  117.7 348.6 all-reduce.1
  551.5 41.6 reduce-scatter.1
where the time goes:
time: 601 us; the launch traced here: 600 us
  waiting for transfers between devices  389 us (65%)
  local copies, waits for them, and re-layouts  97.3 us (16%)
  blocking collectives  46.3 us (8%)
  other arithmetic  30.8 us (5%)
  matrix products  18.6 us (3%)
  between operations  13.7 us (2%)
    psum x1, waiting for transfers between devices, from_root(): return lax.psum(jnp.where(mine, shard, jnp.zeros_like(shard)), axis)  347 us
    all_gather x1, blocking collectives, shards(): requests = lax.all_gather(fetch_list, 'tm', axis=0, tiled=True)  46.3 us
    reduce_scatter x1, waiting for transfers between devices, shards(): lax.psum_scatter(partial_value.astype(jnp.bfloat16), 'head', scatter_dime...  41.8 us
    gather x2, local copies, waits for them, and re-layouts, outgoing(): picked = jnp.take(block_rows, chosen, axis=0)  40.9 us
    gather x2, local copies, waits for them, and re-layouts, attend(): jnp.take(fetched, list_rows, axis=0).reshape(per_step, -1, 2, feature_width)  16.9 us
    slice x2, local copies, waits for them, and re-layouts, attend(): far_keys = picked[:, :, 0].reshape(per_step, -1, head_count, DH)  14.3 us
  transfers between devices with their start and end apart: 3, of which 2 were waited for; matrix products, arithmetic and copies ran while one was open for 2% of the time, Pallas kernels for 0%

commit v1 on v0

--- a/solution.py
+++ b/solution.py
@@ -12,7 +12,7 @@
 
 def from_root(shard, axis, root):
     mine = lax.axis_index(axis) == root
-    return lax.psum(jnp.where(mine, shard, jnp.zeros_like(shard)), axis)
+    return jnp.sum(lax.all_gather(jnp.where(mine, shard, jnp.zeros_like(shard)), axis), axis=0)
 
 
 def owner_ranks(owners):

time: 601 us -> 645 us (1.073)
  other arithmetic: 30.8 us -> 74.4 us
  waiting for transfers between devices: 389 us -> 382 us
    psum x1 -> x0, waiting for transfers between devices: 347 us -> none  [from_root(): return lax.psum(jnp.where(mine, shard, jnp.zeros_like(shard)), axis)]
    all_to_all x1, waiting for transfers between devices: 0.01 us -> 334 us  [shards(): lax.all_to_all(outbound, 'tm', split_axis=0, concat_axis=0, tiled=True)]
    reduce_sum x0 -> x1, other arithmetic: none -> 46.4 us  [from_root(): jnp.sum(lax.all_gather(jnp.where(mine, shard, jnp.zeros_like(shard)), axi...]
    slice x1 -> x2, local copies, waits for them, and re-layouts: 1.49 us -> 10.3 us  [shards(): panel_values = panel_rows[:, 1].reshape(-1, head_count, DH)]
    reduce_scatter x1, waiting for transfers between devices: 41.8 us -> 48.6 us  [shards(): lax.psum_scatter(partial_value.astype(jnp.bfloat16), 'head', scatter_dime...]
  transfers between devices with their start and end apart: 3 -> 3, of which waited for: 2 -> 2; matrix products, arithmetic and copies ran while one was open for 2% -> 18% of each run, Pallas kernels for 0% -> 0%
where the time goes in v1:
time: 645 us; the launch traced here: 644 us
  waiting for transfers between devices  382 us (59%)
  local copies, waits for them, and re-layouts  102 us (16%)
  other arithmetic  74.4 us (12%)
  blocking collectives  46.2 us (7%)
  matrix products  21.2 us (3%)
  between operations  13.7 us (2%)
    all_to_all x1, waiting for transfers between devices, shards(): lax.all_to_all(outbound, 'tm', split_axis=0, concat_axis=0, tiled=True)  334 us
    reduce_scatter x1, waiting for transfers between devices, shards(): lax.psum_scatter(partial_value.astype(jnp.bfloat16), 'head', scatter_dime...  48.6 us
    reduce_sum x1, other arithmetic, from_root(): jnp.sum(lax.all_gather(jnp.where(mine, shard, jnp.zeros_like(shard)), axi...  46.4 us
    all_gather x1, blocking collectives, shards(): requests = lax.all_gather(fetch_list, 'tm', axis=0, tiled=True)  46.2 us
    gather x2, local copies, waits for them, and re-layouts, outgoing(): picked = jnp.take(block_rows, chosen, axis=0)  36.9 us
    gather x2, local copies, waits for them, and re-layouts, attend(): jnp.take(fetched, list_rows, axis=0).reshape(per_step, -1, 2, feature_width)  17.6 us
    slice x2, local copies, waits for them, and re-layouts, attend(): far_keys = picked[:, :, 0].reshape(per_step, -1, head_count, DH)  14.5 us
  transfers between devices with their start and end apart: 3, of which 2 were waited for; matrix products, arithmetic and copies ran while one was open for 18% of the time, Pallas kernels for 0%

profile of v1, /device:TPU:1, one launch (start us, length us, event | category | flops | bytes accessed | tf_op | source)
XLA Modules:
  0.0 644.3 jit_solution(13112777727693959116)
XLA Ops:
  6.5 2.5 broadcast_select_fusion.1
  9.0 0.0 all-gather.4.cloned.1.call-update
  9.0 46.2 %all-gather.1 = s32[32,1,32]{2,1,0:T(1,128)S(1)} all-gather(s32[1,1,32]{2,1,0:T(1,128)} %bitcast.116), channel_id=1, replica_groups=mesh['tm'=32,'head'=4,'rep'=2] {'tm'}, dimensions={0}, use_global_device_ids=true | all-gather | bytes 4224 | tf_op jit(solution)/shard_map/all_gather | solution.py:46
  55.2 0.8 convert_reduce_fusion
  56.0 0.1 select_reduce_fusion
  56.1 0.1 copy.116
  56.3 0.1 fusion.34
  56.4 0.1 copy.115
  56.5 0.1 copy.117
  56.6 0.1 reshape.205
  56.7 29.4 %gather_fusion = bf16[64,128,2,384]{3,2,1,0:T(2,128)(2,1)} fusion(bf16[8,128,2,384]{3,2,1,0:T(2,128)(2,1)} %bitcast.102, s32[1024]{0:T(1024)S(1)} %pad_clamp_fusion.2), kind=kCustom, calls=%fused_computation | custom fusion | bytes 25166080 | tf_op jit(solution)/shard_map/jit(_take)/gather | solution.py:34
  86.1 7.5 %copy.118 = bf16[64,128,2,384]{3,1,2,0:T(8,128)(2,1)S(1)} copy(bf16[64,128,2,384]{3,2,1,0:T(2,128)(2,1)} %gather_fusion) | data formatting | bytes 25165824 | tf_op jit(solution)/shard_map/jit(_take)/gather | solution.py:34
  93.6 6.0 select_select_fusion
  99.6 5.0 all-to-all-start
  104.6 0.0 reduce-scatter.2.cloned.1.call-start
  104.7 0.1 reshape.221
  104.8 0.1 broadcast_bitcast_fusion
  104.9 0.2 copy.122
  105.1 0.1 squeeze.28
  105.3 0.2 convert_reduce_fusion.1
  105.5 0.1 iota_compare_fusion.1
  105.6 333.7 %all-to-all-done = bf16[32,2,128,2,384]{4,2,3,1,0:T(8,128)(2,1)} async-done(((bf16[32,2,128,2,384]{4,2,3,1,0:T(8,128)(2,1)}), bf16[32,2,128,2,384]{4,2,3,1,0:T(8,128)(2,1)}, u32[]{:S(2)}, u32[]{:S(2)}) %all-to-all-start) | async-done | bytes 12582944 | tf_op jit(solution)/shard_map/all_to_all | solution.py:48
  439.3 8.9 %gather_fusion.1 = bf16[32,128,2,384]{3,1,2,0:T(8,128)(2,1)} fusion(bf16[64,128,2,384]{3,1,2,0:T(8,128)(2,1)} %bitcast.7, s32[1024]{0:T(1024)S(1)} %pad_clamp_fusion.1), kind=kCustom, calls=%fused_computation.1 | custom fusion | bytes 12583040 | tf_op jit(solution)/shard_map/jit(_take)/gather | solution.py:50
  448.2 6.2 broadcast_select_fusion
  454.3 10.4 %gather_fusion.2 = bf16[64,128,2,384]{3,1,2,0:T(8,128)(2,1)} fusion(bf16[32,128,2,384]{3,1,2,0:T(8,128)(2,1)} %broadcast_select_fusion, s32[1024]{0:T(1024)S(1)} %pad_clamp_fusion), kind=kCustom, calls=%fused_computation.2 | custom fusion | bytes 25166080 | tf_op jit(solution)/shard_map/while/body/eval_jaxpr/jit(_take)/gather | solution.py:66
  464.7 7.2 %copy.119 = bf16[64,128,2,384]{3,1,0,2:T(8,128)(2,1)S(1)} copy(bf16[64,128,2,384]{3,1,2,0:T(8,128)(2,1)} %gather_fusion.2) | data formatting | bytes 25165824 | tf_op jit(solution)/shard_map/while/body/eval_jaxpr/jit(_take)/gather | solution.py:66
  471.9 3.0 bitcast_select_fusion
  474.9 5.7 fusion.41
  480.6 8.8 %copy.121 = bf16[4,2048,1,384]{1,3,0,2:T(8,128)(2,1)} copy(bf16[4,2048,1,384]{3,1,0,2:T(8,128)(2,1)} %get-tuple-element.23) | data formatting | bytes 12582912 | tf_op jit(solution)/shard_map/while/body/eval_jaxpr/slice | solution.py:67
  489.3 8.8 %copy.120 = bf16[4,2048,1,384]{1,3,0,2:T(8,128)(2,1)} copy(bf16[4,2048,1,384]{3,1,0,2:T(8,128)(2,1)} %get-tuple-element.24) | data formatting | bytes 12582912 | tf_op jit(solution)/shard_map/while/body/eval_jaxpr/slice | solution.py:68
  498.1 9.7 %bitcast_reduce_fusion = (f32[4,3,128]{2,1,0:T(4,128)S(1)}, f32[4,3,2048,128]{3,2,1,0:T(8,128)}) fusion(bf16[4,2048,3,128]{1,3,2,0:T(8,128)(2,1)} %bitcast.109, bf16[4,128,3,128]{1,0,3,2:T(4,128)(2,1)S(1)} %squeeze.28), kind=kOutput, calls=%fused_computation.4 | convolution fusion | flops 811596288 | bytes 19273728 | tf_op jit(solution)/shard_map/while/body/eval_jaxpr/gqhd,gkhd->ghqk/dot_general | solution.py:70
  507.8 46.4 %reduce_sum.68 = bf16[1024,2,384]{2,1,0:T(2,128)(2,1)} reduce(bf16[32,1024,2,384]{3,2,1,0:T(2,128)(2,1)} %bitcast.107, bf16[]{:T(256)} %constant.124.clone.1), dimensions={0}, to_apply=%region_5.6 | reduce | flops 24379392 | bytes 51904512 | tf_op jit(solution)/shard_map/reduce_sum | solution.py:15
  554.1 5.7 fusion.42
  559.8 4.7 copy.131
  564.5 3.5 copy.125
  567.9 0.0 slice-start
  567.9 1.8 fusion.9
  569.8 0.0 slice-start.1
  569.8 2.2 fusion.7
  572.0 0.0 slice-start.2
  572.0 6.8 %fusion.1 = f32[4,3,128]{2,1,0:T(4,128)S(1)} fusion(f32[4,3,2048,128]{3,2,1,0:T(8,128)} %get-tuple-element.43, f32[4,3,128]{2,1,0:T(4,128)S(1)} %copy.129), kind=kLoop, calls=%fused_computation.8 | loop fusion | flops 9435648 | bytes 12595200 | tf_op jit(solution)/shard_map/while/body/eval_jaxpr/reduce_sum | solution.py:84
  578.9 0.0 copy-start.1
  578.9 5.5 fusion.12
  584.4 0.6 fusion.24
  585.1 0.3 copy.134
  585.4 3.5 convolution_convert_fusion
  588.9 0.0 reduce-scatter.2.cloned.1.call-update
  588.9 48.6 %reduce-scatter.2.cloned.1.call-done = bf16[512,768]{1,0:T(8,128)(2,1)} async-done(((bf16[512,3072]{1,0:T(8,128)(2,1)}), bf16[512,768]{1,0:T(8,128)(2,1)}) %reduce-scatter.2.cloned.1.call-update) | async-done | bytes 786448 | tf_op jit(solution)/shard_map/reduce_scatter | solution.py:104
  (36 shorter events, 0.2 us)
Async XLA Ops:
  6.5 578.8 %copy-start = (bf16[384,3072]{1,0:T(8,128)(2,1)S(1)}, bf16[384,3072]{1,0:T(8,128)(2,1)}, u32[]{:S(2)}) copy-start(bf16[384,3072]{1,0:T(8,128)(2,1)} %param.8) | copy-start | bytes 7077892
  6.5 501.3 %all-gather.4.cloned.1.call-start = ((), (), s32[]{:S(2)}) async-start(), calls=%async_computation.3 | async-start | bytes 51904512 | tf_op jit(solution)/shard_map/all_gather | solution.py:15
  99.6 5.1 copy-start.3
  99.6 5.3 copy-start.2
  99.6 5.6 copy-start.4
  99.6 5.8 copy-start.5
  99.6 339.6 %all-to-all-start = ((bf16[32,2,128,2,384]{4,2,3,1,0:T(8,128)(2,1)}), bf16[32,2,128,2,384]{4,2,3,1,0:T(8,128)(2,1)}, u32[]{:S(2)}, u32[]{:S(2)}) async-start(bf16[32,2,128,2,384]{4,2,3,1,0:T(8,128)(2,1)} %select_select_fusion), calls=%async_computation | async-start | bytes 25165824 | tf_op jit(solution)/shard_map/all_to_all | solution.py:48
  104.6 532.9 %reduce-scatter.2.cloned.1.call-start = ((), (), s32[]{:S(2)}) async-start(), calls=%async_computation.2 | async-start | bytes 3932160 | tf_op jit(solution)/shard_map/reduce_scatter | solution.py:104
  567.9 10.9 %slice-start = ((s8[12582912]{0:T(1024)(128)(4,1)}), s8[4194304]{0:T(1024)(128)(4,1)S(1)}, s32[]{:S(2)}) async-start(s8[12582912]{0:T(1024)(128)(4,1)} %bitcast.103), calls=%async_computation.4 | async-start | bytes 8388608
  569.8 9.0 %slice-start.1 = ((s8[12582912]{0:T(1024)(128)(4,1)}), s8[4194304]{0:T(1024)(128)(4,1)S(1)}, s32[]{:S(2)}) async-start(s8[12582912]{0:T(1024)(128)(4,1)} %bitcast.103), calls=%async_computation.5 | async-start | bytes 8388608
  572.0 6.8 %slice-start.2 = ((s8[12582912]{0:T(1024)(128)(4,1)}), s8[4194304]{0:T(1024)(128)(4,1)S(1)}, s32[]{:S(2)}) async-start(s8[12582912]{0:T(1024)(128)(4,1)} %bitcast.103), calls=%async_computation.6 | async-start | bytes 8388608
  578.9 5.6 copy-start.1
Sparse Core Ops, SparseCore 0:
  10.1 490.3 all-gather.3
  589.0 48.3 reduce-scatter.1
